TPU v7x, 256 devices: a whole 4x4x8 slice. The times are simulated.
256 devices in a mesh: dp: 8 (over y, core), expert: 32 (over x, z).
Axes of the slice: x: 4, y: 4, z: 8, core: 2. Of those that a mesh axis runs over, the one named last changes fastest.
Arguments:
- tokens: bfloat16 [32768, 2048], P(('dp', 'expert')), may hold values from -6 to 6
- expert_ids: int32 [32768, 2], P(('dp', 'expert')), may hold values from 0 to 31, all different within a row; in each aligned block of 128 rows (0 to 127, 128 to 255, ...) at most 12 rows name the same one
- upstream: bfloat16 [32768, 2048], P(('dp', 'expert')), may hold values from -6 to 6
- gain: float32 [2048], replicated, may hold values from 0.5 to 1.5
- router: bfloat16 [2048, 32], replicated, may hold values from -0.125 to 0.125
- gate_weight_matrix: bfloat16 [32, 2048, 1024], P('expert', 'dp'), may hold values from -0.125 to 0.125
- up_weight: bfloat16 [32, 2048, 1024], P('expert', 'dp'), may hold values from -0.125 to 0.125
- down_weight: bfloat16 [32, 1024, 2048], P('expert', None, 'dp'), may hold values from -0.1875 to 0.1875
Outputs:
- mixed: bfloat16 [32768, 2048], P(('dp', 'expert'))
- d_tokens: bfloat16 [32768, 2048], P(('dp', 'expert'))
- gate_weight_gradient: bfloat16 [32, 2048, 1024], P('expert', 'dp')
- up_weight_gradient: bfloat16 [32, 2048, 1024], P('expert', 'dp')
- down_weight_gradient: bfloat16 [32, 1024, 2048], P('expert', None, 'dp')
- d_router: float32 [2048, 32], replicated
- d_gain: float32 [2048], replicated
Inputs may be any that keep to these rules, and one draw needn't show every extreme that they name: `expert_ids`: the two experts of a token differ. Among the tokens of one device (aligned blocks of 128 rows) no expert is named more than 12 times, and in some block one expert is named exactly 12 times.
All inputs are finite; a program needn't handle non-finite values.
Results may differ from a plain program's by a relative error of at most 0.014.
Values may be sent and summed in bfloat16 or wider, within the bound.
No kernel may reach another device: no remote copies, remote signals or barrier semaphores. Data moves between devices by JAX's collectives and lax.ppermute only.
A program may use at most 128 MiB of HBM per device.

v0:
```python
import jax
import jax.numpy as jnp
from jax import lax
from jax.sharding import PartitionSpec as P

norm_eps = 1e-06


def slot_layout(expert_ids, experts, capacity):
    flattened = expert_ids.reshape(-1)
    onehot = (flattened[:, None] == jnp.arange(experts, dtype=jnp.int32)[None, :]).astype(jnp.int32)
    ranking = jnp.sum(jnp.cumsum(onehot, axis=0) * onehot, axis=1) - 1
    slot_ids = flattened * capacity + ranking
    sources = (
        jnp.zeros((experts * capacity,), jnp.int32)
        .at[slot_ids]
        .set(jnp.arange(flattened.shape[0], dtype=jnp.int32))
    )
    counts = jnp.sum(onehot, axis=0)
    slots_occupied = (jnp.arange(capacity, dtype=jnp.int32)[None, :] < counts[:, None]).reshape(-1)
    return (slot_ids, sources, slots_occupied)


def transposed_product(left, right):
    return lax.dot_general(
        left, right, (((1,), (1,)), ((), ())), preferred_element_type=jnp.float32
    )


def inner_product(left, right):
    return lax.dot_general(
        left, right, (((0,), (0,)), ((), ())), preferred_element_type=jnp.float32
    )


def on_device(
    tokens, expert_ids, upstream, gain, router, gate_weight_matrix, up_weight, down_weight
):
    experts = lax.axis_size("expert")
    tok_rows = tokens.shape[0]
    width = tokens.shape[1]
    feed = gate_weight_matrix.shape[2]
    capacity = 3 * tok_rows // experts
    source = tokens.astype(jnp.float32)
    inverse = lax.rsqrt(jnp.mean(source * source, axis=-1, keepdims=True) + norm_eps)
    unit_rows = source * inverse
    normed = (unit_rows * gain).astype(jnp.bfloat16)
    scores = jax.nn.sigmoid(jnp.dot(normed, router, preferred_element_type=jnp.float32))
    picked = expert_ids[:, :, None] == jnp.arange(experts, dtype=jnp.int32)[None, None, :]
    chosen = jnp.sum(jnp.where(picked, scores[:, None, :], 0.0), axis=2)
    total = jnp.sum(chosen, axis=1, keepdims=True)
    gates = chosen / total
    slot_ids, sources, slots_occupied = slot_layout(expert_ids, experts, capacity)
    slot_pairs = slot_ids.reshape(tok_rows, 2)
    send_rows = jnp.where(
        slots_occupied[:, None], normed[sources // 2], jnp.zeros((), jnp.bfloat16)
    )
    arrived = lax.all_to_all(
        send_rows.reshape(experts, capacity, width),
        "expert",
        split_axis=0,
        concat_axis=0,
        tiled=True,
    )
    expert_in = arrived.reshape(experts * capacity, width)
    pieces = (
        lax.all_gather(gate_weight_matrix, "dp", axis=1, tiled=True),
        lax.all_gather(up_weight, "dp", axis=1, tiled=True),
    )
    columns = expert_in
    pre_gate = jnp.dot(columns, pieces[0][0], preferred_element_type=jnp.float32)
    pre_up = jnp.dot(columns, pieces[1][0], preferred_element_type=jnp.float32)
    sigma = jax.nn.sigmoid(pre_gate)
    active = pre_gate * sigma
    hidden = (active * pre_up).astype(jnp.bfloat16)
    expert_out = jnp.dot(
        hidden,
        lax.all_gather(down_weight, "dp", axis=2, tiled=True)[0],
        preferred_element_type=jnp.float32,
    ).astype(jnp.bfloat16)
    returned = lax.all_to_all(
        expert_out.reshape(experts, capacity, width),
        "expert",
        split_axis=0,
        concat_axis=0,
        tiled=True,
    )
    outputs = returned.reshape(experts * capacity, width)[slot_pairs].astype(jnp.float32)
    combined = gates[:, :, None] * outputs
    mixed = (source + combined[:, 0] + combined[:, 1]).astype(jnp.bfloat16)
    cotangent = upstream.astype(jnp.float32)
    d_gates = jnp.sum(cotangent[:, None, :] * outputs, axis=2)
    weight_rows = gates.reshape(-1)[sources]
    d_send = jnp.where(
        slots_occupied[:, None], weight_rows[:, None] * cotangent[sources // 2], 0.0
    ).astype(jnp.bfloat16)
    d_arrived = lax.all_to_all(
        d_send.reshape(experts, capacity, width), "expert", split_axis=0, concat_axis=0, tiled=True
    )
    d_out = d_arrived.reshape(experts * capacity, width)
    columns = d_out
    d_hidden = transposed_product(columns, lax.all_gather(down_weight, "dp", axis=2, tiled=True)[0])
    d_pre_gate = (d_hidden * pre_up * sigma * (1.0 + pre_gate * (1.0 - sigma))).astype(jnp.bfloat16)
    d_pre_up = (d_hidden * active).astype(jnp.bfloat16)
    pieces = (
        lax.all_gather(gate_weight_matrix, "dp", axis=1, tiled=True),
        lax.all_gather(up_weight, "dp", axis=1, tiled=True),
    )
    block = transposed_product(d_pre_gate, pieces[0][0]) + transposed_product(
        d_pre_up, pieces[1][0]
    )
    d_rows = block.astype(jnp.bfloat16)
    d_back = lax.all_to_all(
        d_rows.reshape(experts, capacity, width), "expert", split_axis=0, concat_axis=0, tiled=True
    )
    d_parts = d_back.reshape(experts * capacity, width)[slot_pairs].astype(jnp.float32)
    grad_rows = lax.psum_scatter(
        jnp.concatenate(
            [
                inner_product(expert_in, d_pre_gate),
                inner_product(expert_in, d_pre_up),
                inner_product(d_out, hidden),
            ],
            axis=1,
        ).astype(jnp.bfloat16),
        "dp",
        scatter_dimension=0,
        tiled=True,
    ).astype(jnp.float32)
    gate_weight_gradient = grad_rows[:, :feed].astype(jnp.bfloat16)[None]
    up_weight_gradient = grad_rows[:, feed : 2 * feed].astype(jnp.bfloat16)[None]
    down_weight_gradient = grad_rows[:, 2 * feed :].T.astype(jnp.bfloat16)[None]
    blended = jnp.sum(gates * d_gates, axis=1, keepdims=True)
    d_chosen = (d_gates - blended) / total
    d_logit = d_chosen * chosen * (1.0 - chosen)
    d_logits = jnp.sum(jnp.where(picked, d_logit[:, :, None], 0.0), axis=1)
    router_float = router.astype(jnp.float32)
    d_normed = (
        d_parts[:, 0]
        + d_parts[:, 1]
        + jnp.dot(d_logits, router_float.T, precision=lax.Precision.HIGHEST)
    )
    d_unit = d_normed * gain
    inner = jnp.mean(d_unit * unit_rows, axis=-1, keepdims=True)
    d_tokens = (cotangent + inverse * (d_unit - unit_rows * inner)).astype(jnp.bfloat16)
    part_router = jnp.dot(normed.astype(jnp.float32).T, d_logits, precision=lax.Precision.HIGHEST)
    part_gain = jnp.sum(d_normed * unit_rows, axis=0)
    d_router, d_gain = lax.psum((part_router, part_gain), ("dp", "expert"))
    return (
        mixed,
        d_tokens,
        gate_weight_gradient,
        up_weight_gradient,
        down_weight_gradient,
        d_router,
        d_gain,
    )


def solution(mesh):
    return jax.shard_map(
        on_device,
        mesh=mesh,
        in_specs=(
            P(("dp", "expert"), None),
            P(("dp", "expert"), None),
            P(("dp", "expert"), None),
            P(),
            P(),
            P("expert", "dp", None),
            P("expert", "dp", None),
            P("expert", None, "dp"),
        ),
        out_specs=(
            P(("dp", "expert"), None),
            P(("dp", "expert"), None),
            P("expert", "dp", None),
            P("expert", "dp", None),
            P("expert", None, "dp"),
            P(),
            P(),
        ),
        check_vma=False,
    )
```

profile of v0, /device:TPU:2, one launch (start us, length us, event | category | flops | bytes accessed | tf_op | source)
XLA Modules:
  0.0 638.8 jit_solution(4836383149556349928)
XLA Ops:
  13.7 3.1 gather_fusion
  16.8 2.4 gather.20
  19.5 60.0 %all_to_all.20 = bf16[32,12,2048]{2,1,0:T(8,128)(2,1)S(1)} all-to-all(bf16[32,12,2048]{2,1,0:T(8,128)(2,1)S(1)} %broadcast_select_fusion), channel_id=1, replica_groups=mesh['dp'=8,'expert'=32] {'expert'}, dimensions={0} | all-to-all | bytes 3145728 | tf_op jit(solution)/shard_map/all_to_all | solution.py:58
  80.9 5.8 fusion.10
  86.6 5.9 multiply_convert_fusion.2
  92.6 31.3 %all-gather.8.cloned.1.call-done = bf16[1,1024,2048]{2,1,0:T(8,128)(2,1)} async-done(((bf16[1,1024,256]{2,1,0:T(8,128)(2,1)}), bf16[1,1024,2048]{2,1,0:T(8,128)(2,1)}) %all-gather.8.cloned.1.call-update) | async-done | bytes 4194320 | tf_op jit(solution)/shard_map/all_gather | solution.py:78
  123.9 4.2 fusion.14
  129.7 10.3 %all-to-all-start.1 = ((bf16[32,12,2048]{2,1,0:T(8,128)(2,1)}), bf16[32,12,2048]{2,1,0:T(8,128)(2,1)}, u32[]{:S(2)}, u32[]{:S(2)}) async-start(bf16[32,12,2048]{2,1,0:T(8,128)(2,1)} %reshape.197), calls=%async_computation.1 | async-start | bytes 4194304 | tf_op jit(solution)/shard_map/all_to_all | solution.py:81
  140.6 3.3 gather_fusion.3
  143.9 4.6 gather.24
  148.9 39.2 %all-to-all-done.1 = bf16[32,12,2048]{2,1,0:T(8,128)(2,1)} async-done(((bf16[32,12,2048]{2,1,0:T(8,128)(2,1)}), bf16[32,12,2048]{2,1,0:T(8,128)(2,1)}, u32[]{:S(2)}, u32[]{:S(2)}) %all-to-all-start.1) | async-done | bytes 1572896 | tf_op jit(solution)/shard_map/all_to_all | solution.py:81
  188.1 2.5 reshape.198
  190.6 2.4 gather_fusion.1
  193.0 3.4 reshape.257
  196.3 2.6 multiply_reduce_fusion
  199.3 2.8 gather_fusion.2
  202.2 2.6 select_convert_fusion
  204.9 57.8 %all_to_all.21 = bf16[32,12,2048]{2,1,0:T(8,128)(2,1)S(1)} all-to-all(bf16[32,12,2048]{2,1,0:T(8,128)(2,1)S(1)} %select_convert_fusion), channel_id=1, replica_groups=mesh['dp'=8,'expert'=32] {'expert'}, dimensions={0} | all-to-all | bytes 3145728 | tf_op jit(solution)/shard_map/all_to_all | solution.py:97
  264.0 4.1 convolution_convert_fusion
  268.3 2.3 multiply_convert_fusion.1
  270.6 2.4 convolution_convert_fusion.2
  273.0 2.4 convolution_convert_fusion.1
  275.4 21.4 %pad_maximum_fusion = bf16[2048,3072]{0,1:T(8,128)(2,1)} fusion(bf16[2048,1024]{0,1:T(8,128)(2,1)S(1)} %convolution_convert_fusion, bf16[2048,1024]{0,1:T(8,128)(2,1)S(1)} %convolution_convert_fusion.1, bf16[2048,1024]{0,1:T(8,128)(2,1)S(1)} %convolution_convert_fusion.2), kind=kLoop, calls=%fused_computation.6 | loop fusion | flops 37748736 | bytes 25165824 | tf_op jit(solution)/shard_map/concatenate | solution.py:118
  297.9 4.2 fusion.4
  305.5 7.8 %all-to-all-start.3 = ((bf16[32,12,2048]{2,1,0:T(8,128)(2,1)}), bf16[32,12,2048]{2,1,0:T(8,128)(2,1)}, u32[]{:S(2)}, u32[]{:S(2)}) async-start(bf16[32,12,2048]{2,1,0:T(8,128)(2,1)} %reshape.200), calls=%async_computation.3 | async-start | bytes 4194304 | tf_op jit(solution)/shard_map/all_to_all | solution.py:113
  314.4 2.6 copy_multiply_fusion
  317.0 43.3 %all-to-all-done.3 = bf16[32,12,2048]{2,1,0:T(8,128)(2,1)} async-done(((bf16[32,12,2048]{2,1,0:T(8,128)(2,1)}), bf16[32,12,2048]{2,1,0:T(8,128)(2,1)}, u32[]{:S(2)}, u32[]{:S(2)}) %all-to-all-start.3) | async-done | bytes 1572896 | tf_op jit(solution)/shard_map/all_to_all | solution.py:113
  360.3 2.7 reshape.201
  367.4 2.3 fusion.31
  369.7 74.9 %psum.15 = f32[2048]{0:T(1024)} all-reduce(f32[2048]{0:T(1024)S(1)} %get-tuple-element.35), channel_id=1, replica_groups=mesh['dp'=8,'expert'=32] {'dp','expert'}, use_global_device_ids=true, to_apply=%region_15.16 | all-reduce | flops 2048 | bytes 16384 | tf_op jit(solution)/shard_map/psum | solution.py:148
  444.7 2.7 fusion.30
  451.7 178.7 %all-reduce.2.cloned.1.call-done = f32[2048,32]{0,1:T(8,128)} async-done(((f32[2048,32]{0,1:T(8,128)}), f32[2048,32]{0,1:T(8,128)}) %all-reduce.2.cloned.1.call-update) | async-done | bytes 262160 | tf_op jit(solution)/shard_map/psum | solution.py:148
  (102 shorter events, 28.3 us)
Async XLA Ops:
  7.2 141.4 %copy-start = (bf16[2048,32]{0,1:T(8,128)(2,1)S(1)}, bf16[2048,32]{0,1:T(8,128)(2,1)}, u32[]{:S(2)}) copy-start(bf16[2048,32]{0,1:T(8,128)(2,1)} %param.12) | copy-start | bytes 393220
  7.2 6.1 copy-start.3
  7.2 6.3 copy-start.10
  7.2 73.7 %all-gather.4.cloned.1.call-start = ((), (), s32[]{:S(2)}) async-start(), calls=%async_computation.5 | async-start | bytes 4718592 | tf_op jit(solution)/shard_map/all_gather | solution.py:67
  7.9 78.7 %all-gather.6.cloned.1.call-start = ((), (), s32[]{:S(2)}) async-start(), calls=%async_computation.6 | async-start | bytes 4718592 | tf_op jit(solution)/shard_map/all_gather | solution.py:68
  8.7 115.2 %all-gather.8.cloned.1.call-start = ((), (), s32[]{:S(2)}) async-start(), calls=%async_computation.7 | async-start | bytes 4718592 | tf_op jit(solution)/shard_map/all_gather | solution.py:78
  80.9 5.8 copy-start.7
  129.7 10.8 %copy-start.5 = (bf16[128,2048]{1,0:T(8,128)(2,1)S(1)}, bf16[128,2048]{1,0:T(8,128)(2,1)}, u32[]{:S(2)}) copy-start(bf16[128,2048]{1,0:T(8,128)(2,1)} %param.10) | copy-start | bytes 1572868
  129.7 58.4 %all-to-all-start.1 = ((bf16[32,12,2048]{2,1,0:T(8,128)(2,1)}), bf16[32,12,2048]{2,1,0:T(8,128)(2,1)}, u32[]{:S(2)}, u32[]{:S(2)}) async-start(bf16[32,12,2048]{2,1,0:T(8,128)(2,1)} %reshape.197), calls=%async_computation.1 | async-start | bytes 4194304 | tf_op jit(solution)/shard_map/all_to_all | solution.py:81
  140.0 307.4 %reduce-scatter.2.cloned.1.call-start = ((), (), s32[]{:S(2)}) async-start(), calls=%async_computation.8 | async-start | bytes 14155776 | tf_op jit(solution)/shard_map/reduce_scatter | solution.py:117
  143.9 4.9 copy-start.11
  264.0 4.2 copy-start.9
  264.0 4.2 copy-start.13
  264.0 4.2 copy-start.18
  264.0 4.3 copy-start.19
  268.3 2.3 copy-start.8
  270.5 2.4 copy-start.14
  270.6 2.4 copy-start.16
  296.8 1.1 copy-start.17
  297.9 4.2 copy-start.12
  297.9 4.2 copy-start.15
  305.5 8.9 %copy-start.1 = (f32[128,2,2048]{2,1,0:T(2,128)S(1)}, f32[128,2,2048]{2,1,0:T(2,128)}, u32[]{:S(2)}) copy-start(f32[128,2,2048]{2,1,0:T(2,128)} %reshape.257) | copy-start | bytes 6291460
  305.5 54.9 %all-to-all-start.3 = ((bf16[32,12,2048]{2,1,0:T(8,128)(2,1)}), bf16[32,12,2048]{2,1,0:T(8,128)(2,1)}, u32[]{:S(2)}, u32[]{:S(2)}) async-start(bf16[32,12,2048]{2,1,0:T(8,128)(2,1)} %reshape.200), calls=%async_computation.3 | async-start | bytes 4194304 | tf_op jit(solution)/shard_map/all_to_all | solution.py:113
  313.3 317.1 %all-reduce.2.cloned.1.call-start = ((), (), s32[]{:S(2)}) async-start(), calls=%async_computation.9 | async-start | bytes 524288 | tf_op jit(solution)/shard_map/psum | solution.py:148
  365.8 1.7 copy-start.4
  367.4 77.3 %copy-start.2 = (f32[128,2,2048]{2,0,1:T(8,128)S(1)}, f32[128,2,2048]{2,0,1:T(8,128)}, u32[]{:S(2)}) copy-start(f32[128,2,2048]{2,0,1:T(8,128)} %copy_multiply_fusion) | copy-start | bytes 6291460
  367.4 77.3 %copy-start.6 = (bf16[128,2048]{1,0:T(8,128)(2,1)S(1)}, bf16[128,2048]{1,0:T(8,128)(2,1)}, u32[]{:S(2)}) copy-start(bf16[128,2048]{1,0:T(8,128)(2,1)} %param.10) | copy-start | bytes 1572868
Sparse Core Ops, SparseCore 0:
  9.9 37.5 all-gather.3
  49.3 34.5 all-gather.5
  85.8 38.0 all-gather.7
  296.9 73.3 reduce-scatter.1
  376.2 254.0 all-reduce.1
where the time goes:
time: 646 us; the launch traced here: 639 us
  waiting for transfers between devices  295 us (46%)
  blocking collectives  193 us (30%)
  local copies, waits for them, and re-layouts  48 us (7%)
  matrix products  36.7 us (6%)
  other arithmetic  33.7 us (5%)
  starting transfers between devices  18.6 us (3%)
  between operations  14.5 us (2%)
    psum x1, waiting for transfers between devices, on_device(): d_router, d_gain = lax.psum((part_router, part_gain), ('dp', 'expert'))  179 us
    psum x1, blocking collectives, on_device(): d_router, d_gain = lax.psum((part_router, part_gain), ('dp', 'expert'))  74.9 us
    all_to_all x1, blocking collectives, on_device(): lax.all_to_all(send_rows.reshape(experts, capacity, width), 'expert', spl...  60 us
    all_to_all x1, blocking collectives, on_device(): lax.all_to_all(d_send.reshape(experts, capacity, width), 'expert', split_...  57.8 us
    all_to_all x1, waiting for transfers between devices, on_device(): lax.all_to_all(d_rows.reshape(experts, capacity, width), 'expert', split_...  43.3 us
    all_to_all x1, waiting for transfers between devices, on_device(): lax.all_to_all(expert_out.reshape(experts, capacity, width), 'expert', sp...  39.2 us
    all_gather x1, waiting for transfers between devices, on_device(): lax.all_gather(down_weight, 'dp', axis=2, tiled=True)[0]  31.3 us
    concatenate x1, other arithmetic, on_device(): jnp.concatenate([inner_product(expert_in, d_pre_gate), inner_product(expe...  21.4 us
  transfers between devices with their start and end apart: 7, of which 4 were waited for; matrix products, arithmetic and copies ran while one was open for 9% of the time, Pallas kernels for 0%

commit v1 on v0

--- a/solution.py
+++ b/solution.py
@@ -36,6 +36,10 @@
 def on_device(
     tokens, expert_ids, upstream, gain, router, gate_weight_matrix, up_weight, down_weight
 ):
+
+    def load_turns(array_in):
+        return lax.psum(lax.psum(array_in, axis_name="dp"), axis_name="expert")
+
     experts = lax.axis_size("expert")
     tok_rows = tokens.shape[0]
     width = tokens.shape[1]
@@ -145,7 +149,7 @@
     d_tokens = (cotangent + inverse * (d_unit - unit_rows * inner)).astype(jnp.bfloat16)
     part_router = jnp.dot(normed.astype(jnp.float32).T, d_logits, precision=lax.Precision.HIGHEST)
     part_gain = jnp.sum(d_normed * unit_rows, axis=0)
-    d_router, d_gain = lax.psum((part_router, part_gain), ("dp", "expert"))
+    d_router, d_gain = load_turns((part_router, part_gain))
     return (
         mixed,
         d_tokens,

time: 646 us -> 536 us (0.83)
  waiting for transfers between devices: 295 us -> 226 us
  blocking collectives: 193 us -> 139 us
  starting transfers between devices: 18.6 us -> 29.3 us
    psum x1 -> x2, waiting for transfers between devices: 179 us -> 62.7 us  [load_turns(): return lax.psum(lax.psum(array_in, axis_name='dp'), axis_name='expert')]
    all_to_all x1 -> x0, blocking collectives: 57.8 us -> none  [on_device(): lax.all_to_all(d_send.reshape(experts, capacity, width), 'expert', split_...]
    all_to_all x0 -> x1, waiting for transfers between devices: none -> 45.8 us  [on_device(): lax.all_to_all(d_send.reshape(experts, capacity, width), 'expert', split_...]
    all_to_all x0 -> x1, starting transfers between devices: none -> 8.84 us  [on_device(): lax.all_to_all(d_send.reshape(experts, capacity, width), 'expert', split_...]
    psum x1 -> x2, blocking collectives: 74.9 us -> 79 us  [load_turns(): return lax.psum(lax.psum(array_in, axis_name='dp'), axis_name='expert')]
  transfers between devices with their start and end apart: 7 -> 9, of which waited for: 4 -> 5; matrix products, arithmetic and copies ran while one was open for 9% -> 18% of each run, Pallas kernels for 0% -> 0%
where the time goes in v1:
time: 536 us; the launch traced here: 528 us
  waiting for transfers between devices  226 us (42%)
  blocking collectives  139 us (26%)
  local copies, waits for them, and re-layouts  46.7 us (9%)
  matrix products  37 us (7%)
  other arithmetic  35 us (7%)
  starting transfers between devices  29.3 us (5%)
  between operations  14.8 us (3%)
    psum x2, blocking collectives, load_turns(): return lax.psum(lax.psum(array_in, axis_name='dp'), axis_name='expert')  79 us
    psum x2, waiting for transfers between devices, load_turns(): return lax.psum(lax.psum(array_in, axis_name='dp'), axis_name='expert')  62.7 us
    all_to_all x1, blocking collectives, on_device(): lax.all_to_all(send_rows.reshape(experts, capacity, width), 'expert', spl...  60 us
    all_to_all x1, waiting for transfers between devices, on_device(): lax.all_to_all(d_send.reshape(experts, capacity, width), 'expert', split_...  45.8 us
    all_to_all x1, waiting for transfers between devices, on_device(): lax.all_to_all(d_rows.reshape(experts, capacity, width), 'expert', split_...  44.6 us
    all_to_all x1, waiting for transfers between devices, on_device(): lax.all_to_all(expert_out.reshape(experts, capacity, width), 'expert', sp...  39.4 us
    all_gather x1, waiting for transfers between devices, on_device(): lax.all_gather(down_weight, 'dp', axis=2, tiled=True)[0]  31.2 us
    concatenate x1, other arithmetic, on_device(): jnp.concatenate([inner_product(expert_in, d_pre_gate), inner_product(expe...  21.4 us
  transfers between devices with their start and end apart: 9, of which 5 were waited for; matrix products, arithmetic and copies ran while one was open for 18% of the time, Pallas kernels for 0%

profile of v1, /device:TPU:2, one launch (start us, length us, event | category | flops | bytes accessed | tf_op | source)
XLA Modules:
  0.0 527.7 jit_solution(10643675346765394318)
XLA Ops:
  13.7 3.1 gather_fusion
  16.8 2.4 gather.20
  19.5 60.0 %all_to_all.20 = bf16[32,12,2048]{2,1,0:T(8,128)(2,1)S(1)} all-to-all(bf16[32,12,2048]{2,1,0:T(8,128)(2,1)S(1)} %broadcast_select_fusion), channel_id=1, replica_groups=mesh['dp'=8,'expert'=32] {'expert'}, dimensions={0} | all-to-all | bytes 3145728 | tf_op jit(solution)/shard_map/all_to_all | solution.py:62
  80.9 5.8 %fusion.10 = f32[384,1024]{1,0:T(8,128)} fusion(bf16[384,2048]{1,0:T(8,128)(2,1)} %reshape.196, bf16[1,2048,1024]{2,1,0:T(8,128)(2,1)} %all-gather.4.cloned.1.call-done), kind=kOutput, calls=%fused_computation.17 | convolution fusion | flops 1610612736 | bytes 7340032 | tf_op jit(solution)/shard_map/dot_general | solution.py:75
  86.6 6.0 %multiply_convert_fusion.2 = (bf16[384,1024]{1,0:T(8,128)(2,1)}, f32[384,1024]{1,0:T(8,128)}) fusion(f32[384,1024]{1,0:T(8,128)} %fusion.10, bf16[384,2048]{1,0:T(8,128)(2,1)S(1)} %copy-done.7, bf16[1,2048,1024]{2,1,0:T(8,128)(2,1)} %all-gather.6.cloned.1.call-done), kind=kOutput, calls=%fused_computation.31 | convolution fusion | flops 1612972032 | bytes 9699328 | tf_op jit(solution)/shard_map/dot_general | solution.py:76
  92.6 31.2 %all-gather.8.cloned.1.call-done = bf16[1,1024,2048]{2,1,0:T(8,128)(2,1)} async-done(((bf16[1,1024,256]{2,1,0:T(8,128)(2,1)}), bf16[1,1024,2048]{2,1,0:T(8,128)(2,1)}) %all-gather.8.cloned.1.call-update) | async-done | bytes 4194320 | tf_op jit(solution)/shard_map/all_gather | solution.py:82
  123.9 4.2 fusion.14
  129.7 10.8 %all-to-all-start.1 = ((bf16[32,12,2048]{2,1,0:T(8,128)(2,1)}), bf16[32,12,2048]{2,1,0:T(8,128)(2,1)}, u32[]{:S(2)}, u32[]{:S(2)}) async-start(bf16[32,12,2048]{2,1,0:T(8,128)(2,1)} %reshape.197), calls=%async_computation.1 | async-start | bytes 4194304 | tf_op jit(solution)/shard_map/all_to_all | solution.py:85
  140.7 3.3 gather_fusion.3
  144.0 4.6 gather.24
  148.9 39.4 %all-to-all-done.1 = bf16[32,12,2048]{2,1,0:T(8,128)(2,1)} async-done(((bf16[32,12,2048]{2,1,0:T(8,128)(2,1)}), bf16[32,12,2048]{2,1,0:T(8,128)(2,1)}, u32[]{:S(2)}, u32[]{:S(2)}) %all-to-all-start.1) | async-done | bytes 1572896 | tf_op jit(solution)/shard_map/all_to_all | solution.py:85
  188.3 2.5 reshape.198
  193.2 3.4 reshape.257
  196.6 2.6 multiply_reduce_fusion
  199.5 2.8 gather_fusion.2
  202.5 4.0 select_convert_fusion
  206.5 8.8 %all-to-all-start.2 = ((bf16[32,12,2048]{2,1,0:T(8,128)(2,1)}), bf16[32,12,2048]{2,1,0:T(8,128)(2,1)S(1)}, u32[]{:S(2)}, u32[]{:S(2)}) async-start(bf16[32,12,2048]{2,1,0:T(8,128)(2,1)} %select_convert_fusion), calls=%async_computation.2 | async-start | bytes 4194304 | tf_op jit(solution)/shard_map/all_to_all | solution.py:101
  217.0 45.8 %all-to-all-done.2 = bf16[32,12,2048]{2,1,0:T(8,128)(2,1)S(1)} async-done(((bf16[32,12,2048]{2,1,0:T(8,128)(2,1)}), bf16[32,12,2048]{2,1,0:T(8,128)(2,1)S(1)}, u32[]{:S(2)}, u32[]{:S(2)}) %all-to-all-start.2) | async-done | bytes 1572896 | tf_op jit(solution)/shard_map/all_to_all | solution.py:101
  264.2 4.1 convolution_convert_fusion
  270.7 2.4 convolution_convert_fusion.2
  273.2 2.4 convolution_convert_fusion.1
  275.6 21.4 %pad_maximum_fusion = bf16[2048,3072]{0,1:T(8,128)(2,1)} fusion(bf16[2048,1024]{0,1:T(8,128)(2,1)S(1)} %convolution_convert_fusion, bf16[2048,1024]{0,1:T(8,128)(2,1)S(1)} %convolution_convert_fusion.1, bf16[2048,1024]{0,1:T(8,128)(2,1)S(1)} %convolution_convert_fusion.2), kind=kLoop, calls=%fused_computation.6 | loop fusion | flops 37748736 | bytes 25165824 | tf_op jit(solution)/shard_map/concatenate | solution.py:122
  297.0 4.2 fusion.4
  304.6 8.9 %all-to-all-start.3 = ((bf16[32,12,2048]{2,1,0:T(8,128)(2,1)}), bf16[32,12,2048]{2,1,0:T(8,128)(2,1)}, u32[]{:S(2)}, u32[]{:S(2)}) async-start(bf16[32,12,2048]{2,1,0:T(8,128)(2,1)} %reshape.200), calls=%async_computation.3 | async-start | bytes 4194304 | tf_op jit(solution)/shard_map/all_to_all | solution.py:117
  313.5 2.6 copy_multiply_fusion
  316.2 44.6 %all-to-all-done.3 = bf16[32,12,2048]{2,1,0:T(8,128)(2,1)} async-done(((bf16[32,12,2048]{2,1,0:T(8,128)(2,1)}), bf16[32,12,2048]{2,1,0:T(8,128)(2,1)}, u32[]{:S(2)}, u32[]{:S(2)}) %all-to-all-start.3) | async-done | bytes 1572896 | tf_op jit(solution)/shard_map/all_to_all | solution.py:117
  360.8 2.7 reshape.201
  367.9 2.4 fusion.31
  370.3 13.1 %psum.30 = f32[2048]{0:T(1024)S(1)} all-reduce(f32[2048]{0:T(1024)S(1)} %get-tuple-element.35), channel_id=1, replica_groups=mesh['dp'=8,'expert'=32] {'dp'}, use_global_device_ids=true, to_apply=%region_16.17 | all-reduce | flops 2048 | bytes 16384 | tf_op jit(solution)/shard_map/psum | solution.py:41
  383.3 65.9 %psum.31 = f32[2048]{0:T(1024)} all-reduce(f32[2048]{0:T(1024)S(1)} %psum.30), channel_id=1, replica_groups=mesh['dp'=8,'expert'=32] {'expert'}, use_global_device_ids=true, to_apply=%region_17.18 | all-reduce | flops 2048 | bytes 16384 | tf_op jit(solution)/shard_map/psum | solution.py:41
  449.3 2.7 fusion.30
  456.2 62.7 %all-reduce.5.cloned.1.call-done = f32[2048,32]{0,1:T(8,128)} async-done(((f32[2048,32]{0,1:T(8,128)}), f32[2048,32]{0,1:T(8,128)}) %all-reduce.5.cloned.1.call-update) | async-done | bytes 262160 | tf_op jit(solution)/shard_map/psum | solution.py:41
  (99 shorter events, 32.1 us)
Async XLA Ops:
  7.2 141.4 %copy-start = (bf16[2048,32]{0,1:T(8,128)(2,1)S(1)}, bf16[2048,32]{0,1:T(8,128)(2,1)}, u32[]{:S(2)}) copy-start(bf16[2048,32]{0,1:T(8,128)(2,1)} %param.12) | copy-start | bytes 393220
  7.2 6.1 %copy-start.3 = (bf16[128,2048]{1,0:T(8,128)(2,1)S(1)}, bf16[128,2048]{1,0:T(8,128)(2,1)}, u32[]{:S(2)}) copy-start(bf16[128,2048]{1,0:T(8,128)(2,1)} %param.8) | copy-start | bytes 1572868
  7.2 6.3 %copy-start.10 = (f32[2048]{0:T(1024)S(1)}, f32[2048]{0:T(1024)}, u32[]{:S(2)}) copy-start(f32[2048]{0:T(1024)} %param.11) | copy-start | bytes 24580
  7.2 73.7 %all-gather.4.cloned.1.call-start = ((), (), s32[]{:S(2)}) async-start(), calls=%async_computation.5 | async-start | bytes 4718592 | tf_op jit(solution)/shard_map/all_gather | solution.py:71
  7.9 78.7 %all-gather.6.cloned.1.call-start = ((), (), s32[]{:S(2)}) async-start(), calls=%async_computation.6 | async-start | bytes 4718592 | tf_op jit(solution)/shard_map/all_gather | solution.py:72
  8.7 115.2 %all-gather.8.cloned.1.call-start = ((), (), s32[]{:S(2)}) async-start(), calls=%async_computation.7 | async-start | bytes 4718592 | tf_op jit(solution)/shard_map/all_gather | solution.py:82
  80.9 5.8 %copy-start.7 = (bf16[384,2048]{1,0:T(8,128)(2,1)S(1)}, bf16[384,2048]{1,0:T(8,128)(2,1)}, u32[]{:S(2)}) copy-start(bf16[384,2048]{1,0:T(8,128)(2,1)} %reshape.196) | copy-start | bytes 4718596
  129.7 11.0 %copy-start.5 = (bf16[128,2048]{1,0:T(8,128)(2,1)S(1)}, bf16[128,2048]{1,0:T(8,128)(2,1)}, u32[]{:S(2)}) copy-start(bf16[128,2048]{1,0:T(8,128)(2,1)} %param.10) | copy-start | bytes 1572868
  129.7 58.7 %all-to-all-start.1 = ((bf16[32,12,2048]{2,1,0:T(8,128)(2,1)}), bf16[32,12,2048]{2,1,0:T(8,128)(2,1)}, u32[]{:S(2)}, u32[]{:S(2)}) async-start(bf16[32,12,2048]{2,1,0:T(8,128)(2,1)} %reshape.197), calls=%async_computation.1 | async-start | bytes 4194304 | tf_op jit(solution)/shard_map/all_to_all | solution.py:85
  144.0 4.9 copy-start.11
  206.5 56.4 %all-to-all-start.2 = ((bf16[32,12,2048]{2,1,0:T(8,128)(2,1)}), bf16[32,12,2048]{2,1,0:T(8,128)(2,1)S(1)}, u32[]{:S(2)}, u32[]{:S(2)}) async-start(bf16[32,12,2048]{2,1,0:T(8,128)(2,1)} %select_convert_fusion), calls=%async_computation.2 | async-start | bytes 4194304 | tf_op jit(solution)/shard_map/all_to_all | solution.py:101
  215.3 100.8 %all-reduce.3.cloned.1.call-start = ((), (), s32[]{:S(2)}) async-start(), calls=%async_computation.9 | async-start | bytes 524288 | tf_op jit(solution)/shard_map/psum | solution.py:41
  216.5 235.5 %reduce-scatter.2.cloned.1.call-start = ((), (), s32[]{:S(2)}) async-start(), calls=%async_computation.8 | async-start | bytes 14155776 | tf_op jit(solution)/shard_map/reduce_scatter | solution.py:121
  264.2 4.2 copy-start.9
  264.2 4.2 copy-start.13
  264.2 4.2 copy-start.14
  264.2 4.3 copy-start.15
  268.4 2.3 copy-start.8
  297.0 4.2 copy-start.12
  304.6 8.9 %copy-start.1 = (f32[128,2,2048]{2,1,0:T(2,128)S(1)}, f32[128,2,2048]{2,1,0:T(2,128)}, u32[]{:S(2)}) copy-start(f32[128,2,2048]{2,1,0:T(2,128)} %reshape.257) | copy-start | bytes 6291460
  304.6 56.2 %all-to-all-start.3 = ((bf16[32,12,2048]{2,1,0:T(8,128)(2,1)}), bf16[32,12,2048]{2,1,0:T(8,128)(2,1)}, u32[]{:S(2)}, u32[]{:S(2)}) async-start(bf16[32,12,2048]{2,1,0:T(8,128)(2,1)} %reshape.200), calls=%async_computation.3 | async-start | bytes 4194304 | tf_op jit(solution)/shard_map/all_to_all | solution.py:117
  313.5 205.5 %all-reduce.5.cloned.1.call-start = ((), (), s32[]{:S(2)}) async-start(), calls=%async_computation.10 | async-start | bytes 524288 | tf_op jit(solution)/shard_map/psum | solution.py:41
  366.2 1.7 copy-start.4
  367.8 81.4 %copy-start.2 = (f32[128,2,2048]{2,0,1:T(8,128)S(1)}, f32[128,2,2048]{2,0,1:T(8,128)}, u32[]{:S(2)}) copy-start(f32[128,2,2048]{2,0,1:T(8,128)} %copy_multiply_fusion) | copy-start | bytes 6291460
  367.8 81.4 %copy-start.6 = (bf16[128,2048]{1,0:T(8,128)(2,1)S(1)}, bf16[128,2048]{1,0:T(8,128)(2,1)}, u32[]{:S(2)}) copy-start(bf16[128,2048]{1,0:T(8,128)(2,1)} %param.10) | copy-start | bytes 1572868
Sparse Core Ops, SparseCore 0:
  9.9 37.5 all-gather.3
  49.3 34.5 all-gather.5
  85.8 38.0 all-gather.7
  218.7 66.7 all-reduce.2
  297.1 74.4 reduce-scatter.1
  374.9 143.9 all-reduce.4
